TPU v7x, 32 devices: a whole 2x2x4 slice. The times are simulated.
32 devices in a mesh: groups: 2 (over x), seq: 16 (over z, y, core).
Axes of the slice: x: 2, y: 2, z: 4, core: 2. Of those that a mesh axis runs over, the one named last changes fastest.
Arguments:
- features: bfloat16 [4096, 2048], P(('groups', 'seq')), parts along dimension 0, may hold values from -40 to 40
- state_write: bfloat16 [4096, 64], P(('groups', 'seq')), parts along dimension 0, may hold values from -0.75 to 0.75
- state_read: bfloat16 [4096, 64], P(('groups', 'seq')), parts along dimension 0, may hold values from -0.75 to 0.75
- log_decay: float32 [4096, 32], P(('groups', 'seq')), parts along dimension 0, may hold values from -2 to 0
- skip_gain: float32 [32], replicated, may hold values from 1 to 4
- post_gain: float32 [2048], replicated, may hold values from 0.5 to 2
- start_index: int32 [4096], P(('groups', 'seq')), parts along dimension 0, may hold values from 0 to 2047, as said below
- step_noise: bfloat16 [3, 4096, 1024], P(None, ('groups', 'seq')), parts along dimension 1, may hold values from -4 to 4
- act_weight: bfloat16 [2048, 128], replicated, may hold values from -0.125 to 0.125
- dyn_weight: bfloat16 [2048, 1024], replicated, may hold values from -0.125 to 0.125
- act_in_weight: bfloat16 [128, 1024], replicated, may hold values from -0.5 to 0.5
- out_weight: bfloat16 [1024, 2048], replicated, may hold values from -0.1875 to 0.1875
- value_weight: bfloat16 [1024], replicated, may hold values from -0.1875 to 0.1875
Outputs:
- posterior: bfloat16 [4096, 2048], P(('groups', 'seq')), parts along dimension 0
- values: float32 [3, 4096], P(None, ('groups', 'seq')), parts along dimension 1
- final_latent: bfloat16 [4096, 2048], P(('groups', 'seq')), parts along dimension 0
There are 2 independent parts, one for each index of `groups`. A program takes and returns all parts, laid end to end along the dimension named above; an argument that names none is the same for every part. Nothing has to cross between parts.
Inputs may be any that keep to these rules, and one draw needn't show every extreme that they name: `start_index`: each aligned block of 128 starts (the starts of one device) names exactly 8 time steps in every aligned range of 128 time steps.
All inputs are finite; a program needn't handle non-finite values.
Results may differ from a plain program's by a relative error of at most 0.01.
Values may be sent and summed in bfloat16 or wider, within the bound.
No kernel may reach another device: no remote copies, remote signals or barrier semaphores. Data moves between devices by JAX's collectives and lax.ppermute only.
A program may use at most 192 MiB of HBM per device.

v0:
```python
import jax
import jax.numpy as jnp
from jax import lax
from jax.sharding import PartitionSpec as P


def entering(shard, axis, combine, identity):
    count, mine = (lax.axis_size(axis), lax.axis_index(axis))
    everything = jax.tree.map(lambda part: lax.all_gather(part, axis), shard)
    start = jax.tree.map(
        lambda part, zero: jnp.broadcast_to(jnp.asarray(zero, part.dtype), part.shape),
        shard,
        identity,
    )

    def lap(k, before):
        reached = k < mine
        new = combine(before, jax.tree.map(lambda part: part[k], everything))
        return jax.tree.map(lambda a, b: jnp.where(reached, a, b), new, before)

    return lax.fori_loop(0, count, lap, start)


def lower_ones(count):
    positions = jnp.arange(count, dtype=jnp.int32)
    return (positions[:, None] >= positions[None, :]).astype(jnp.float32)


def local_pass(wide_in, write_in, read_in, decay_in):
    row_count, width = wide_in.shape
    head_count = decay_in.shape[1]
    head_width = width // head_count
    block = min(256, row_count)
    block_count = row_count // block
    positions = jnp.arange(block, dtype=jnp.int32)
    lower_mask = positions[:, None] >= positions[None, :]
    lower_table = lower_mask.astype(jnp.float32)

    def advance(state_now, inputs):
        x_block, write_block, read_block, decay_block = inputs
        running = jnp.dot(lower_table, decay_block, precision=lax.Precision.HIGHEST)
        running_t = running.T
        spread = running_t[:, :, None] - running_t[:, None, :]
        weight = jnp.exp(jnp.where(lower_mask[None], spread, -jnp.inf))
        gram = jnp.dot(read_block, write_block.T, preferred_element_type=jnp.float32)
        inner_part = jnp.einsum(
            "hts,shp->thp",
            weight * gram[None],
            x_block.reshape(block, head_count, head_width),
            precision=lax.Precision.HIGHEST,
        ).reshape(block, width)
        read_wide = read_block.astype(jnp.float32)
        carried = jnp.dot(read_wide, state_now, precision=lax.Precision.HIGHEST) * jnp.repeat(
            jnp.exp(running), head_width, axis=1
        )
        tail = jnp.repeat(jnp.exp(running[-1:] - running), head_width, axis=1)
        whole_decay = jnp.repeat(jnp.exp(running[-1]), head_width)
        added = jnp.einsum(
            "sn,sd->nd",
            write_block.astype(jnp.float32),
            x_block * tail,
            precision=lax.Precision.HIGHEST,
        )
        state_next = state_now * whole_decay[None, :] + added
        return (state_next, inner_part + carried)

    zero_state = jnp.zeros((write_in.shape[1], width), jnp.float32)
    inputs = (
        wide_in.reshape(block_count, block, width),
        write_in.reshape(block_count, block, write_in.shape[1]),
        read_in.reshape(block_count, block, read_in.shape[1]),
        decay_in.reshape(block_count, block, head_count),
    )
    end_state, outputs = lax.scan(advance, zero_state, inputs)
    return (end_state, outputs.reshape(row_count, width))


def join_states(earlier, later):
    grow = jnp.repeat(later[0], earlier[1].shape[1] // later[0].shape[0])
    return (earlier[0] * later[0], earlier[1] * grow[None, :] + later[1])


def regroup_rows(posterior, start_index):
    row_count = posterior.shape[0]
    peer_count = lax.axis_size("seq")
    start_count = start_index.shape[0]
    slot_cap = start_count // peer_count
    owners = start_index // row_count
    offset = start_index % row_count
    owner_hits = (owners[:, None] == jnp.arange(peer_count, dtype=jnp.int32)[None, :]).astype(
        jnp.float32
    )
    running_hits = jnp.dot(lower_ones(start_count), owner_hits, precision=lax.Precision.HIGHEST)
    slot_rank = jnp.sum(running_hits * owner_hits, axis=1).astype(jnp.int32) - 1
    slot_index = owners * slot_cap + slot_rank
    wanted = (
        jnp.zeros((peer_count * slot_cap,), jnp.int32)
        .at[slot_index]
        .set(offset)
        .reshape(peer_count, slot_cap)
    )
    picked = jnp.take(
        posterior, lax.all_to_all(wanted, "seq", split_axis=0, concat_axis=0, tiled=True), axis=0
    )
    landed = lax.all_to_all(picked, "seq", split_axis=0, concat_axis=0, tiled=True)
    return jnp.take(landed.reshape(peer_count * slot_cap, posterior.shape[1]), slot_index, axis=0)


def imagine(latent, step_noise, act_weight, dyn_weight, act_in_weight, out_weight, value_weight):
    value_list = []
    for step_idx in range(step_noise.shape[0]):
        wide = latent.astype(jnp.float32)
        normed = (wide * lax.rsqrt(jnp.mean(wide * wide, axis=-1, keepdims=True) + 1e-06)).astype(
            jnp.bfloat16
        )
        action = jnp.tanh(jnp.dot(normed, act_weight, preferred_element_type=jnp.float32)).astype(
            jnp.bfloat16
        )
        inner = jnp.dot(normed, dyn_weight, preferred_element_type=jnp.float32) + jnp.dot(
            action, act_in_weight, preferred_element_type=jnp.float32
        )
        hidden = (jax.nn.silu(inner) + step_noise[step_idx].astype(jnp.float32)).astype(
            jnp.bfloat16
        )
        value_list.append(jnp.dot(hidden, value_weight, preferred_element_type=jnp.float32))
        latent = (wide + jnp.dot(hidden, out_weight, preferred_element_type=jnp.float32)).astype(
            jnp.bfloat16
        )
    return (jnp.stack(value_list), latent)


def per_device(
    features,
    state_write,
    state_read,
    log_decay,
    skip_gain,
    post_gain,
    start_index,
    step_noise,
    act_weight,
    dyn_weight,
    act_in_weight,
    out_weight,
    value_weight,
):
    row_count, width = features.shape
    head_count = log_decay.shape[1]
    head_width = width // head_count
    wide_in = features.astype(jnp.float32)
    end_state, local_out = local_pass(wide_in, state_write, state_read, log_decay)
    shard_decay = jnp.exp(jnp.sum(log_decay, axis=0))
    identity = (jnp.ones((head_count,), jnp.float32), jnp.zeros_like(end_state))
    _, carry_in = entering((shard_decay, end_state), "seq", join_states, identity)
    entered = jnp.exp(jnp.dot(lower_ones(row_count), log_decay, precision=lax.Precision.HIGHEST))
    from_before = jnp.dot(
        state_read.astype(jnp.float32), carry_in, precision=lax.Precision.HIGHEST
    ) * jnp.repeat(entered, head_width, axis=1)
    mixed = local_out + from_before + jnp.repeat(skip_gain, head_width)[None, :] * wide_in
    head_table = (
        jnp.arange(width, dtype=jnp.int32)[:, None] // head_width
        == jnp.arange(head_count, dtype=jnp.int32)[None, :]
    ).astype(jnp.float32)
    square_mean = jnp.dot(mixed * mixed, head_table, precision=lax.Precision.HIGHEST) / head_width
    scale = jnp.repeat(lax.rsqrt(square_mean + 1e-05), head_width, axis=1)
    posterior = (mixed * scale * post_gain[None, :]).astype(jnp.bfloat16)
    latent = regroup_rows(posterior, start_index)
    values, final_latent = imagine(
        latent, step_noise, act_weight, dyn_weight, act_in_weight, out_weight, value_weight
    )
    return (posterior, values, final_latent)


def solution(mesh):
    placed = (
        P(("groups", "seq"), None),
        P(("groups", "seq"), None),
        P(("groups", "seq"), None),
        P(("groups", "seq"), None),
        P(),
        P(),
        P(("groups", "seq")),
        P(None, ("groups", "seq"), None),
        P(),
        P(),
        P(),
        P(),
        P(),
    )
    return jax.shard_map(
        per_device,
        mesh=mesh,
        in_specs=placed,
        out_specs=(
            P(("groups", "seq"), None),
            P(None, ("groups", "seq")),
            P(("groups", "seq"), None),
        ),
        check_vma=False,
    )
```

profile of v0, /device:TPU:0, one launch (start us, length us, event | category | flops | bytes accessed | tf_op | source)
XLA Modules:
  0.0 165.3 jit_solution(9370423981715717801)
XLA Ops:
  8.7 1.3 copy.32
  10.1 2.3 %fusion.11 = f32[64,2048]{1,0:T(8,128)} fusion(bf16[128,64]{0,1:T(8,128)(2,1)} %param.16, f32[128,2048]{0,1:T(8,128)S(1)} %bitcast.98, bf16[128,2048]{0,1:T(8,128)(2,1)S(1)} %copy.32, f32[2048]{0:T(1024)S(1)} %mul.144), kind=kOutput, calls=%fused_computation.22 | convolution fusion | flops 201981952 | bytes 2121728 | tf_op jit(solution)/shard_map/while/body/eval_jaxpr/sn,sd->nd/dot_general | solution.py:58
  14.3 7.4 %all-to-all-start = ((s32[16,1,8]{2,1,0:T(1,128)}), s32[16,1,8]{2,1,0:T(1,128)S(1)}, u32[]{:S(2)}, u32[]{:S(2)}) async-start(s32[16,1,8]{2,1,0:T(1,128)} %bitcast.12), calls=%async_computation | async-start | bytes 16384 | tf_op jit(solution)/shard_map/all_to_all | solution.py:103
  23.5 2.5 %fusion.12 = f32[32,128,64]{1,2,0:T(8,128)S(1)} fusion(bf16[128,32,64]{0,2,1:T(8,128)(2,1)S(1)} %bitcast.97, f32[128,128]{1,0:T(8,128)S(1)} %fusion.53, f32[32,128]{1,0:T(8,128)S(1)} %bitcast.101, pred[128,128]{1,0:T(8,128)(4,1)S(1)} %iota_compare_fusion.2), kind=kOutput, calls=%fused_computation.23 | convolution fusion | flops 404226048 | bytes 1671168 | tf_op jit(solution)/shard_map/while/body/eval_jaxpr/hts,shp->thp/dot_general | solution.py:46
  26.0 1.6 fusion.5
  27.7 35.1 %all-reduce = f32[512]{0:T(512)S(1)} all-reduce(f32[512]{0:T(512)S(1)} %exponential_dynamic-update-slice_fusion), channel_id=2, replica_groups=mesh['groups'=2,'seq'=16] {'seq'}, use_global_device_ids=true, to_apply=%add | all-reduce | flops 512 | bytes 4096
  63.4 26.4 %all-gather.4.cloned.1.call-done = f32[1024,2048]{1,0:T(8,128)} async-done(((f32[64,2048]{1,0:T(8,128)}), f32[1024,2048]{1,0:T(8,128)}) %all-gather.4.cloned.1.call-update) | async-done | bytes 8388624 | tf_op jit(solution)/shard_map/all_gather | solution.py:9
  89.8 26.5 %while.9 = (s32[]{:T(128)}, f32[64,2048]{1,0:T(8,128)S(1)}, s32[]{:T(128)}, f32[16,32]{1,0:T(8,128)S(1)}, f32[16,64,2048]{2,1,0:T(8,128)}, /*index=5*/s32[]{:T(128)}, s32[]{:T(128)}) while((s32[]{:T(128)}, f32[64,2048]{1,0:T(8,128)S(1)}, s32[]{:T(128)}, f32[16,32]{1,0:T(8,128)S(1)}, f32[16,64,2048]{2,1,0:T(8,128)}, ...), condition=%wide.region_2.3_spmd.clone, body=%wide.region_1.2_spmd.clone.sunk | while | flops 524292 | bytes 1606121 | solution.py:21
  89.9 1.5 fusion.87
  91.6 1.5 fusion.87
  93.2 1.5 fusion.87
  94.9 1.5 fusion.87
  96.5 1.5 fusion.87
  98.2 1.5 fusion.87
  99.9 1.5 fusion.87
  101.5 1.5 fusion.87
  103.2 1.5 fusion.87
  104.8 1.5 fusion.87
  106.5 1.5 fusion.87
  108.1 1.5 fusion.87
  109.8 1.5 fusion.87
  111.5 1.5 fusion.87
  113.1 1.5 fusion.87
  114.8 1.5 fusion.87
  116.3 2.5 %fusion.3 = f32[128,2048]{0,1:T(8,128)S(1)} fusion(f32[128,2048]{0,1:T(8,128)} %fusion.5, f32[128,2048]{0,1:T(8,128)S(1)} %bitcast.96, f32[64,2048]{1,0:T(8,128)S(1)} %get-tuple-element.124, bf16[128,64]{0,1:T(8,128)(2,1)S(1)} %copy-done.8, bf16[128,2048]{0,1:T(8,128)(2,1)S(1)} %copy.32, f32[2048]{0:T(1024)S(1)} %mul.148), kind=kOutput, calls=%fused_computation.12 | convolution fusion | flops 202637312 | bytes 4218880 | tf_op jit(solution)/shard_map/dot_general | solution.py:156
  118.8 1.3 fusion.24
  122.6 3.8 %all-to-all-start.1 = ((bf16[16,8,2048]{2,1,0:T(8,128)(2,1)}), bf16[16,8,2048]{2,1,0:T(8,128)(2,1)S(1)}, u32[]{:S(2)}, u32[]{:S(2)}) async-start(bf16[16,8,2048]{2,1,0:T(8,128)(2,1)} %bitcast_select_fusion), calls=%async_computation.1 | async-start | bytes 1048576 | tf_op jit(solution)/shard_map/all_to_all | solution.py:105
  126.4 14.0 %all-to-all-done.1 = bf16[16,8,2048]{2,1,0:T(8,128)(2,1)S(1)} async-done(((bf16[16,8,2048]{2,1,0:T(8,128)(2,1)}), bf16[16,8,2048]{2,1,0:T(8,128)(2,1)S(1)}, u32[]{:S(2)}, u32[]{:S(2)}) %all-to-all-start.1) | async-done | bytes 524320 | tf_op jit(solution)/shard_map/all_to_all | solution.py:105
  142.2 3.3 %fusion.38 = bf16[128,1024]{1,0:T(8,128)(2,1)S(1)} fusion(f32[128,1024]{1,0:T(8,128)S(1)} %fusion.22, bf16[2048,1024]{1,0:T(8,128)(2,1)} %param.24, bf16[3,128,1024]{2,1,0:T(8,128)(2,1)} %param.22, f32[128]{0:T(128)S(1)} %add_rsqrt_fusion.2, bf16[128,2048]{1,0:T(8,128)(2,1)S(1)} %gather_fusion.1, pred[128]{0:T(512)(128)(4,1)S(1)} %get-tuple-element.162), kind=kOutput, calls=%fused_computation.70 | convolution fusion | flops 538968064 | bytes 5767808 | tf_op jit(solution)/shard_map/dot_general | solution.py:119
  147.2 3.3 %fusion.37 = bf16[128,1024]{1,0:T(8,128)(2,1)S(1)} fusion(f32[128,1024]{1,0:T(8,128)S(1)} %fusion.21, bf16[2048,1024]{1,0:T(8,128)(2,1)} %param.24, bf16[3,128,1024]{2,1,0:T(8,128)(2,1)} %param.22, f32[128,2048]{1,0:T(8,128)S(1)} %get-tuple-element.169, f32[128]{0:T(128)S(1)} %add_rsqrt_fusion.1), kind=kOutput, calls=%fused_computation.68 | convolution fusion | flops 538443776 | bytes 6291968 | tf_op jit(solution)/shard_map/dot_general | solution.py:119
  152.2 3.3 %fusion.36 = bf16[128,1024]{1,0:T(8,128)(2,1)S(1)} fusion(f32[128,1024]{1,0:T(8,128)S(1)} %fusion.20, bf16[2048,1024]{1,0:T(8,128)(2,1)} %param.24, bf16[3,128,1024]{2,1,0:T(8,128)(2,1)} %param.22, f32[128,2048]{1,0:T(8,128)S(1)} %get-tuple-element.171, f32[128]{0:T(128)S(1)} %add_rsqrt_fusion), kind=kOutput, calls=%fused_computation.66 | convolution fusion | flops 538443776 | bytes 6291968 | tf_op jit(solution)/shard_map/dot_general | solution.py:119
  155.8 1.6 fusion.10
  (134 shorter events, 16.4 us)
Async XLA Ops:
  7.2 134.5 %copy-start = (bf16[2048,128]{1,0:T(8,128)(2,1)S(1)}, bf16[2048,128]{1,0:T(8,128)(2,1)}, u32[]{:S(2)}) copy-start(bf16[2048,128]{1,0:T(8,128)(2,1)} %param.23) | copy-start | bytes 1572868
  7.2 14.7 %copy-start.15 = (u32[32]{0:T(128)S(1)}, u32[32]{0:T(128)}, u32[]{:S(2)}) copy-start(u32[32]{0:T(128)} %constant.141) | copy-start | bytes 388
  7.2 14.5 %copy-start.10 = (f32[128,32]{0,1:T(8,128)S(1)}, f32[128,32]{0,1:T(8,128)}, u32[]{:S(2)}) copy-start(f32[128,32]{0,1:T(8,128)} %param.18) | copy-start | bytes 49156
  7.2 16.1 %copy-start.9 = (bf16[128,64]{0,1:T(8,128)(2,1)S(1)}, bf16[128,64]{0,1:T(8,128)(2,1)}, u32[]{:S(2)}) copy-start(bf16[128,64]{0,1:T(8,128)(2,1)} %param.16) | copy-start | bytes 49156
  7.2 5.2 %copy-start.14 = (s32[128]{0:T(128)S(1)}, s32[128]{0:T(128)}, u32[]{:S(2)}) copy-start(s32[128]{0:T(128)} %param.21) | copy-start | bytes 1540
  7.2 16.0 %copy-start.8 = (bf16[128,64]{0,1:T(8,128)(2,1)S(1)}, bf16[128,64]{0,1:T(8,128)(2,1)}, u32[]{:S(2)}) copy-start(bf16[128,64]{0,1:T(8,128)(2,1)} %param.17) | copy-start | bytes 49156
  7.2 82.5 %all-gather.4.cloned.1.call-start = ((), (), s32[]{:S(2)}) async-start(), calls=%async_computation.2 | async-start | bytes 8912896 | tf_op jit(solution)/shard_map/all_gather | solution.py:9
  12.4 50.5 %copy-start.13 = (f32[32]{0:T(128)S(1)}, f32[32]{0:T(128)}, u32[]{:S(2)}) copy-start(f32[32]{0:T(128)} %param.19) | copy-start | bytes 388
  14.3 48.7 %all-to-all-start = ((s32[16,1,8]{2,1,0:T(1,128)}), s32[16,1,8]{2,1,0:T(1,128)S(1)}, u32[]{:S(2)}, u32[]{:S(2)}) async-start(s32[16,1,8]{2,1,0:T(1,128)} %bitcast.12), calls=%async_computation | async-start | bytes 16384 | tf_op jit(solution)/shard_map/all_to_all | solution.py:103
  116.3 3.8 %copy-start.11 = (f32[2048]{0:T(1024)S(1)}, f32[2048]{0:T(1024)}, u32[]{:S(2)}) copy-start(f32[2048]{0:T(1024)} %param.20) | copy-start | bytes 24580
  120.5 5.9 %copy-start.12 = (bf16[1024]{0:T(1024)(128)(2,1)S(1)}, bf16[1024]{0:T(1024)(128)(2,1)}, u32[]{:S(2)}) copy-start(bf16[1024]{0:T(1024)(128)(2,1)} %param.27) | copy-start | bytes 6148
  120.7 20.6 %copy-start.1 = (bf16[128,2048]{1,0:T(8,128)(2,1)}, bf16[128,2048]{1,0:T(8,128)(2,1)S(1)}, u32[]{:S(2)}) copy-start(bf16[128,2048]{1,0:T(8,128)(2,1)S(1)} %copy.40) | copy-start | bytes 1572868
  121.6 20.0 %copy-start.5 = (bf16[128,1024]{1,0:T(8,128)(2,1)S(1)}, bf16[128,1024]{1,0:T(8,128)(2,1)}, u32[]{:S(2)}) copy-start(bf16[128,1024]{1,0:T(8,128)(2,1)} %param.25) | copy-start | bytes 786436
  122.6 17.8 %all-to-all-start.1 = ((bf16[16,8,2048]{2,1,0:T(8,128)(2,1)}), bf16[16,8,2048]{2,1,0:T(8,128)(2,1)S(1)}, u32[]{:S(2)}, u32[]{:S(2)}) async-start(bf16[16,8,2048]{2,1,0:T(8,128)(2,1)} %bitcast_select_fusion), calls=%async_computation.1 | async-start | bytes 1048576 | tf_op jit(solution)/shard_map/all_to_all | solution.py:105
  142.2 3.5 %copy-start.2 = (bf16[1024,2048]{1,0:T(8,128)(2,1)S(1)}, bf16[1024,2048]{1,0:T(8,128)(2,1)}, u32[]{:S(2)}) copy-start(bf16[1024,2048]{1,0:T(8,128)(2,1)} %param.26) | copy-start | bytes 12582916
  147.2 3.5 %copy-start.3 = (bf16[1024,2048]{1,0:T(8,128)(2,1)S(1)}, bf16[1024,2048]{1,0:T(8,128)(2,1)}, u32[]{:S(2)}) copy-start(bf16[1024,2048]{1,0:T(8,128)(2,1)} %param.26) | copy-start | bytes 12582916
  150.8 0.9 copy-start.6
  152.2 3.5 %copy-start.4 = (bf16[1024,2048]{1,0:T(8,128)(2,1)S(1)}, bf16[1024,2048]{1,0:T(8,128)(2,1)}, u32[]{:S(2)}) copy-start(bf16[1024,2048]{1,0:T(8,128)(2,1)} %param.26) | copy-start | bytes 12582916
  155.8 1.7 %copy-start.7 = (bf16[128,1024]{1,0:T(8,128)(2,1)S(1)}, bf16[128,1024]{1,0:T(8,128)(2,1)}, u32[]{:S(2)}) copy-start(bf16[128,1024]{1,0:T(8,128)(2,1)} %copy-done.6) | copy-start | bytes 786436
Sparse Core Ops, SparseCore 0:
  12.5 77.1 all-gather.3
where the time goes:
time: 167 us; the launch traced here: 165 us
  waiting for transfers between devices  40.4 us (24%)
  blocking collectives  35.1 us (21%)
  matrix products  27 us (16%)
  other arithmetic  26.2 us (16%)
  between operations  15.1 us (9%)
  starting transfers between devices  11.2 us (7%)
  local copies, waits for them, and re-layouts  9.99 us (6%)
    unnamed x1, blocking collectives  35.1 us
    all_gather x1, waiting for transfers between devices, entering(): everything = jax.tree.map(lambda part: lax.all_gather(part, axis), shard)  26.4 us
    select_n x16, other arithmetic, lap(): return jax.tree.map(lambda a, b: jnp.where(reached, a, b), new, before)  23.7 us
    all_to_all x1, waiting for transfers between devices, regroup_rows(): lax.all_to_all(picked, 'seq', split_axis=0, concat_axis=0, tiled=True)  14 us
    dot_general x3, matrix products, imagine(): jnp.dot(normed, dyn_weight, preferred_element_type=jnp.float32)  9.93 us
    all_to_all x1, starting transfers between devices, regroup_rows(): lax.all_to_all(wanted, 'seq', split_axis=0, concat_axis=0, tiled=True)  7.41 us
    all_to_all x1, starting transfers between devices, regroup_rows(): lax.all_to_all(picked, 'seq', split_axis=0, concat_axis=0, tiled=True)  3.75 us
    dot_general x3, matrix products, imagine(): jnp.dot(hidden, out_weight, preferred_element_type=jnp.float32)  3.44 us
  transfers between devices with their start and end apart: 3, of which 2 were waited for; matrix products, arithmetic and copies ran while one was open for 4% of the time, Pallas kernels for 0%

commit v1 on v0

--- a/solution.py
+++ b/solution.py
@@ -2,6 +2,18 @@
 import jax.numpy as jnp
 from jax import lax
 from jax.sharding import PartitionSpec as P
+
+
+def in_blocks(shard, dim, devices):
+    lengths = shard.shape
+    pieces = shard.reshape(*lengths[:dim], devices, lengths[dim] // devices, *lengths[dim + 1 :])
+    return jnp.moveaxis(pieces, dim, 0)
+
+
+def joined_along(parts, dim):
+    parts = jnp.moveaxis(parts, 0, dim)
+    lengths = parts.shape
+    return parts.reshape(*lengths[:dim], lengths[dim] * lengths[dim + 1], *lengths[dim + 2 :])
 
 
 def entering(shard, axis, combine, identity):
@@ -102,7 +114,15 @@
     picked = jnp.take(
         posterior, lax.all_to_all(wanted, "seq", split_axis=0, concat_axis=0, tiled=True), axis=0
     )
-    landed = lax.all_to_all(picked, "seq", split_axis=0, concat_axis=0, tiled=True)
+    size, position = (lax.axis_size("seq"), lax.axis_index("seq"))
+    blocks = in_blocks(picked, 0, size)
+    filled = blocks
+    for step in range(1, size):
+        target, source = ((position + step) % size, (position - step) % size)
+        sent = lax.dynamic_index_in_dim(blocks, target, 0)
+        partner_block = lax.ppermute(sent, "seq", [(i, (i + step) % size) for i in range(size)])
+        filled = lax.dynamic_update_slice_in_dim(filled, partner_block, source, axis=0)
+    landed = joined_along(filled, 0)
     return jnp.take(landed.reshape(peer_count * slot_cap, posterior.shape[1]), slot_index, axis=0)
 
 

time: 167 us -> 172 us (1.030)
  starting transfers between devices: 11.2 us -> 28.1 us
  waiting for transfers between devices: 40.4 us -> 29.5 us
    ppermute x0 -> x15, starting transfers between devices: none -> 20.6 us  [regroup_rows(): lax.ppermute(sent, 'seq', [(i, (i + step) % size) for i in range(size)])]
    all_to_all x1 -> x0, waiting for transfers between devices: 14 us -> none  [regroup_rows(): lax.all_to_all(picked, 'seq', split_axis=0, concat_axis=0, tiled=True)]
    all_to_all x1 -> x0, starting transfers between devices: 3.75 us -> none  [regroup_rows(): lax.all_to_all(picked, 'seq', split_axis=0, concat_axis=0, tiled=True)]
    ppermute x0 -> x15, waiting for transfers between devices: none -> 3.51 us  [regroup_rows(): lax.ppermute(sent, 'seq', [(i, (i + step) % size) for i in range(size)])]
  transfers between devices with their start and end apart: 3 -> 17, of which waited for: 2 -> 4; matrix products, arithmetic and copies ran while one was open for 4% -> 4% of each run, Pallas kernels for 0% -> 0%
where the time goes in v1:
time: 172 us; the launch traced here: 171 us
  blocking collectives  35.1 us (20%)
  waiting for transfers between devices  29.5 us (17%)
  starting transfers between devices  28.1 us (16%)
  matrix products  27 us (16%)
  other arithmetic  25.5 us (15%)
  between operations  15.7 us (9%)
  local copies, waits for them, and re-layouts  10.2 us (6%)
    unnamed x1, blocking collectives  35.1 us
    all_gather x1, waiting for transfers between devices, entering(): everything = jax.tree.map(lambda part: lax.all_gather(part, axis), shard)  25.9 us
    select_n x16, other arithmetic, lap(): return jax.tree.map(lambda a, b: jnp.where(reached, a, b), new, before)  23.7 us
    ppermute x15, starting transfers between devices, regroup_rows(): lax.ppermute(sent, 'seq', [(i, (i + step) % size) for i in range(size)])  20.6 us
    dot_general x3, matrix products, imagine(): jnp.dot(normed, dyn_weight, preferred_element_type=jnp.float32)  9.93 us
    all_to_all x1, starting transfers between devices, regroup_rows(): lax.all_to_all(wanted, 'seq', split_axis=0, concat_axis=0, tiled=True)  7.41 us
    ppermute x15, waiting for transfers between devices, regroup_rows(): lax.ppermute(sent, 'seq', [(i, (i + step) % size) for i in range(size)])  3.51 us
  transfers between devices with their start and end apart: 17, of which 4 were waited for; matrix products, arithmetic and copies ran while one was open for 4% of the time, Pallas kernels for 0%

profile of v1, /device:TPU:0, one launch (start us, length us, event | category | flops | bytes accessed | tf_op | source)
XLA Modules:
  0.0 171.3 jit_solution(8304268656404585611)
XLA Ops:
  10.1 2.3 %fusion.11 = f32[64,2048]{1,0:T(8,128)} fusion(bf16[128,64]{0,1:T(8,128)(2,1)} %param.16, f32[128,2048]{0,1:T(8,128)S(1)} %bitcast.130, bf16[128,2048]{0,1:T(8,128)(2,1)S(1)} %copy.34, f32[2048]{0:T(1024)S(1)} %mul.144), kind=kOutput, calls=%fused_computation.22 | convolution fusion | flops 201981952 | bytes 2121728 | tf_op jit(solution)/shard_map/while/body/eval_jaxpr/sn,sd->nd/dot_general | solution.py:70
  14.3 7.4 %all-to-all-start = ((s32[16,1,8]{2,1,0:T(1,128)}), s32[16,1,8]{2,1,0:T(1,128)S(1)}, u32[]{:S(2)}, u32[]{:S(2)}) async-start(s32[16,1,8]{2,1,0:T(1,128)} %bitcast.12), calls=%async_computation | async-start | bytes 16384 | tf_op jit(solution)/shard_map/all_to_all | solution.py:115
  23.8 35.1 %all-reduce = f32[512]{0:T(512)S(1)} all-reduce(f32[512]{0:T(512)S(1)} %exponential_dynamic-update-slice_fusion), channel_id=2, replica_groups=mesh['groups'=2,'seq'=16] {'seq'}, use_global_device_ids=true, to_apply=%add | all-reduce | flops 512 | bytes 4096
  59.4 2.5 %fusion.12 = f32[32,128,64]{1,2,0:T(8,128)S(1)} fusion(bf16[128,32,64]{0,2,1:T(8,128)(2,1)S(1)} %bitcast.129, f32[128,128]{1,0:T(8,128)S(1)} %fusion.53, f32[32,128]{1,0:T(8,128)S(1)} %bitcast.133, pred[128,128]{1,0:T(8,128)(4,1)S(1)} %iota_compare_fusion.2), kind=kOutput, calls=%fused_computation.23 | convolution fusion | flops 404226048 | bytes 1671168 | tf_op jit(solution)/shard_map/while/body/eval_jaxpr/hts,shp->thp/dot_general | solution.py:58
  62.0 1.6 fusion.5
  63.9 25.9 %all-gather.4.cloned.1.call-done = f32[1024,2048]{1,0:T(8,128)} async-done(((f32[64,2048]{1,0:T(8,128)}), f32[1024,2048]{1,0:T(8,128)}) %all-gather.4.cloned.1.call-update) | async-done | bytes 8388624 | tf_op jit(solution)/shard_map/all_gather | solution.py:21
  89.9 26.5 %while.9 = (s32[]{:T(128)}, f32[64,2048]{1,0:T(8,128)S(1)}, s32[]{:T(128)}, f32[16,32]{1,0:T(8,128)S(1)}, f32[16,64,2048]{2,1,0:T(8,128)}, /*index=5*/s32[]{:T(128)}, s32[]{:T(128)}) while((s32[]{:T(128)}, f32[64,2048]{1,0:T(8,128)S(1)}, s32[]{:T(128)}, f32[16,32]{1,0:T(8,128)S(1)}, f32[16,64,2048]{2,1,0:T(8,128)}, ...), condition=%wide.region_2.3_spmd.clone, body=%wide.region_1.2_spmd.clone.sunk | while | flops 524292 | bytes 1606121 | solution.py:33
  91.7 1.5 fusion.87
  93.3 1.5 fusion.87
  95.0 1.5 fusion.87
  96.7 1.5 fusion.87
  98.3 1.5 fusion.87
  100.0 1.5 fusion.87
  101.6 1.5 fusion.87
  103.3 1.5 fusion.87
  105.0 1.5 fusion.87
  106.6 1.5 fusion.87
  109.9 1.5 fusion.87
  114.9 1.5 fusion.87
  116.4 2.5 %fusion.3 = f32[128,2048]{0,1:T(8,128)S(1)} fusion(f32[128,2048]{0,1:T(8,128)} %fusion.5, f32[128,2048]{0,1:T(8,128)S(1)} %bitcast.128, f32[64,2048]{1,0:T(8,128)S(1)} %get-tuple-element.124, bf16[128,64]{0,1:T(8,128)(2,1)S(1)} %copy-done.8, bf16[128,2048]{0,1:T(8,128)(2,1)S(1)} %copy.34, f32[2048]{0:T(1024)S(1)} %mul.148), kind=kOutput, calls=%fused_computation.12 | convolution fusion | flops 202637312 | bytes 4218880 | tf_op jit(solution)/shard_map/dot_general | solution.py:176
  123.0 2.0 %collective-permute-start.2 = (bf16[1,1,8,2048]{3,2,0,1:T(8,128)(2,1)S(1)}, bf16[1,1,8,2048]{3,2,0,1:T(8,128)(2,1)S(1)}, u32[]{:S(2)}, u32[]{:S(2)}) collective-permute-start(bf16[1,1,8,2048]{3,2,0,1:T(8,128)(2,1)S(1)} %get-tuple-element.176), channel_id=1, source_target_pairs={{0,3},{1,4},{2,5},{3,6},{4,7},{5,8},{6,9},{7,10},{8,11},{9,12},{10... | collective-permute-start | bytes 98312 | tf_op jit(solution)/shard_map/ppermute | solution.py:123
  126.2 1.9 %collective-permute-done = bf16[1,1,8,2048]{3,2,0,1:T(8,128)(2,1)S(1)} collective-permute-done((bf16[1,1,8,2048]{3,2,0,1:T(8,128)(2,1)S(1)}, bf16[1,1,8,2048]{3,2,0,1:T(8,128)(2,1)S(1)}, u32[]{:S(2)}, u32[]{:S(2)}) %collective-permute-start) | collective-permute-done | bytes 32800 | tf_op jit(solution)/shard_map/ppermute | solution.py:123
  129.1 2.7 %collective-permute-start.6 = (bf16[1,1,8,2048]{3,2,0,1:T(8,128)(2,1)S(1)}, bf16[1,1,8,2048]{3,2,0,1:T(8,128)(2,1)S(1)}, u32[]{:S(2)}, u32[]{:S(2)}) collective-permute-start(bf16[1,1,8,2048]{3,2,0,1:T(8,128)(2,1)S(1)} %get-tuple-element.172), channel_id=1, source_target_pairs={{0,7},{1,8},{2,9},{3,10},{4,11},{5,12},{6,13},{7,14},{8,15},{9,0},... | collective-permute-start | bytes 98312 | tf_op jit(solution)/shard_map/ppermute | solution.py:123
  131.8 1.8 %collective-permute-start.7 = (bf16[1,1,8,2048]{3,2,0,1:T(8,128)(2,1)S(1)}, bf16[1,1,8,2048]{3,2,0,1:T(8,128)(2,1)S(1)}, u32[]{:S(2)}, u32[]{:S(2)}) collective-permute-start(bf16[1,1,8,2048]{3,2,0,1:T(8,128)(2,1)S(1)} %get-tuple-element.171), channel_id=1, source_target_pairs={{0,8},{1,9},{2,10},{3,11},{4,12},{5,13},{6,14},{7,15},{8,0},{9,1},... | collective-permute-start | bytes 98312 | tf_op jit(solution)/shard_map/ppermute | solution.py:123
  135.2 3.6 %collective-permute-start.10 = (bf16[1,1,8,2048]{3,2,0,1:T(8,128)(2,1)S(1)}, bf16[1,1,8,2048]{3,2,0,1:T(8,128)(2,1)S(1)}, u32[]{:S(2)}, u32[]{:S(2)}) collective-permute-start(bf16[1,1,8,2048]{3,2,0,1:T(8,128)(2,1)S(1)} %get-tuple-element.168), channel_id=1, source_target_pairs={{0,11},{1,12},{2,13},{3,14},{4,15},{5,0},{6,1},{7,2},{8,3},{9,4},{... | collective-permute-start | bytes 98312 | tf_op jit(solution)/shard_map/ppermute | solution.py:123
  140.1 2.0 %collective-permute-start.13 = (bf16[1,1,8,2048]{3,2,0,1:T(8,128)(2,1)S(1)}, bf16[1,1,8,2048]{3,2,0,1:T(8,128)(2,1)S(1)}, u32[]{:S(2)}, u32[]{:S(2)}) collective-permute-start(bf16[1,1,8,2048]{3,2,0,1:T(8,128)(2,1)S(1)} %get-tuple-element.165), channel_id=1, source_target_pairs={{0,14},{1,15},{2,0},{3,1},{4,2},{5,3},{6,4},{7,5},{8,6},{9,7},{10,... | collective-permute-start | bytes 98312 | tf_op jit(solution)/shard_map/ppermute | solution.py:123
  142.1 2.7 %collective-permute-start.14 = (bf16[1,1,8,2048]{3,2,0,1:T(8,128)(2,1)S(1)}, bf16[1,1,8,2048]{3,2,0,1:T(8,128)(2,1)S(1)}, u32[]{:S(2)}, u32[]{:S(2)}) collective-permute-start(bf16[1,1,8,2048]{3,2,0,1:T(8,128)(2,1)S(1)} %get-tuple-element.164), channel_id=1, source_target_pairs={{0,15},{1,0},{2,1},{3,2},{4,3},{5,4},{6,5},{7,6},{8,7},{9,8},{10,9... | collective-permute-start | bytes 98312 | tf_op jit(solution)/shard_map/ppermute | solution.py:123
  144.9 1.5 collective-permute-done.14
  148.2 3.3 %fusion.38 = bf16[128,1024]{1,0:T(8,128)(2,1)S(1)} fusion(f32[128,1024]{1,0:T(8,128)S(1)} %fusion.22, bf16[2048,1024]{1,0:T(8,128)(2,1)} %param.24, bf16[3,128,1024]{2,1,0:T(8,128)(2,1)} %param.22, f32[128]{0:T(128)S(1)} %add_rsqrt_fusion.2, bf16[128,2048]{1,0:T(8,128)(2,1)S(1)} %gather_fusion.1, pred[128]{0:T(512)(128)(4,1)S(1)} %get-tuple-element.162), kind=kOutput, calls=%fused_computation.70 | convolution fusion | flops 538968064 | bytes 5767808 | tf_op jit(solution)/shard_map/dot_general | solution.py:139
  153.3 3.3 %fusion.37 = bf16[128,1024]{1,0:T(8,128)(2,1)S(1)} fusion(f32[128,1024]{1,0:T(8,128)S(1)} %fusion.21, bf16[2048,1024]{1,0:T(8,128)(2,1)} %param.24, bf16[3,128,1024]{2,1,0:T(8,128)(2,1)} %param.22, f32[128,2048]{1,0:T(8,128)S(1)} %get-tuple-element.184, f32[128]{0:T(128)S(1)} %add_rsqrt_fusion.1), kind=kOutput, calls=%fused_computation.68 | convolution fusion | flops 538443776 | bytes 6291968 | tf_op jit(solution)/shard_map/dot_general | solution.py:139
  158.2 3.3 %fusion.36 = bf16[128,1024]{1,0:T(8,128)(2,1)S(1)} fusion(f32[128,1024]{1,0:T(8,128)S(1)} %fusion.20, bf16[2048,1024]{1,0:T(8,128)(2,1)} %param.24, bf16[3,128,1024]{2,1,0:T(8,128)(2,1)} %param.22, f32[128,2048]{1,0:T(8,128)S(1)} %get-tuple-element.186, f32[128]{0:T(128)S(1)} %add_rsqrt_fusion), kind=kOutput, calls=%fused_computation.66 | convolution fusion | flops 538443776 | bytes 6291968 | tf_op jit(solution)/shard_map/dot_general | solution.py:139
  161.8 1.6 fusion.10
  (179 shorter events, 30.5 us)
Async XLA Ops:
  7.2 140.5 %copy-start = (bf16[2048,128]{1,0:T(8,128)(2,1)S(1)}, bf16[2048,128]{1,0:T(8,128)(2,1)}, u32[]{:S(2)}) copy-start(bf16[2048,128]{1,0:T(8,128)(2,1)} %param.23) | copy-start | bytes 1572868
  7.2 15.2 %copy-start.15 = (u32[32]{0:T(128)S(1)}, u32[32]{0:T(128)}, u32[]{:S(2)}) copy-start(u32[32]{0:T(128)} %constant.355) | copy-start | bytes 388
  7.2 15.0 %copy-start.10 = (f32[128,32]{0,1:T(8,128)S(1)}, f32[128,32]{0,1:T(8,128)}, u32[]{:S(2)}) copy-start(f32[128,32]{0,1:T(8,128)} %param.18) | copy-start | bytes 49156
  7.2 52.0 %copy-start.9 = (bf16[128,64]{0,1:T(8,128)(2,1)S(1)}, bf16[128,64]{0,1:T(8,128)(2,1)}, u32[]{:S(2)}) copy-start(bf16[128,64]{0,1:T(8,128)(2,1)} %param.16) | copy-start | bytes 49156
  7.2 5.2 %copy-start.14 = (s32[128]{0:T(128)S(1)}, s32[128]{0:T(128)}, u32[]{:S(2)}) copy-start(s32[128]{0:T(128)} %param.21) | copy-start | bytes 1540
  7.2 51.7 %copy-start.13 = (f32[32]{0:T(128)S(1)}, f32[32]{0:T(128)}, u32[]{:S(2)}) copy-start(f32[32]{0:T(128)} %param.19) | copy-start | bytes 388
  7.2 51.8 %copy-start.12 = (bf16[1024]{0:T(1024)(128)(2,1)S(1)}, bf16[1024]{0:T(1024)(128)(2,1)}, u32[]{:S(2)}) copy-start(bf16[1024]{0:T(1024)(128)(2,1)} %param.27) | copy-start | bytes 6148
  7.2 51.9 %copy-start.8 = (bf16[128,64]{0,1:T(8,128)(2,1)S(1)}, bf16[128,64]{0,1:T(8,128)(2,1)}, u32[]{:S(2)}) copy-start(bf16[128,64]{0,1:T(8,128)(2,1)} %param.17) | copy-start | bytes 49156
  7.3 82.6 %all-gather.4.cloned.1.call-start = ((), (), s32[]{:S(2)}) async-start(), calls=%async_computation.1 | async-start | bytes 8912896 | tf_op jit(solution)/shard_map/all_gather | solution.py:21
  14.3 49.3 %all-to-all-start = ((s32[16,1,8]{2,1,0:T(1,128)}), s32[16,1,8]{2,1,0:T(1,128)S(1)}, u32[]{:S(2)}, u32[]{:S(2)}) async-start(s32[16,1,8]{2,1,0:T(1,128)} %bitcast.12), calls=%async_computation | async-start | bytes 16384 | tf_op jit(solution)/shard_map/all_to_all | solution.py:115
  116.4 3.8 %copy-start.11 = (f32[2048]{0:T(1024)S(1)}, f32[2048]{0:T(1024)}, u32[]{:S(2)}) copy-start(f32[2048]{0:T(1024)} %param.20) | copy-start | bytes 24580
  120.8 21.3 %copy-start.1 = (bf16[128,2048]{1,0:T(8,128)(2,1)}, bf16[128,2048]{1,0:T(8,128)(2,1)S(1)}, u32[]{:S(2)}) copy-start(bf16[128,2048]{1,0:T(8,128)(2,1)S(1)} %copy.43) | copy-start | bytes 1572868
  121.9 25.8 %copy-start.5 = (bf16[128,1024]{1,0:T(8,128)(2,1)S(1)}, bf16[128,1024]{1,0:T(8,128)(2,1)}, u32[]{:S(2)}) copy-start(bf16[128,1024]{1,0:T(8,128)(2,1)} %param.25) | copy-start | bytes 786436
  122.0 6.1 %collective-permute-start = (bf16[1,1,8,2048]{3,2,0,1:T(8,128)(2,1)S(1)}, bf16[1,1,8,2048]{3,2,0,1:T(8,128)(2,1)S(1)}, u32[]{:S(2)}, u32[]{:S(2)}) collective-permute-start(bf16[1,1,8,2048]{3,2,0,1:T(8,128)(2,1)S(1)} %get-tuple-element.178), channel_id=1, source_target_pairs={{0,1},{1,2},{2,3},{3,4},{4,5},{5,6},{6,7},{7,8},{8,9},{9,10},{10,1... | collective-permute-start | bytes 98312 | tf_op jit(solution)/shard_map/ppermute | solution.py:123
  122.4 6.7 %collective-permute-start.1 = (bf16[1,1,8,2048]{3,2,0,1:T(8,128)(2,1)S(1)}, bf16[1,1,8,2048]{3,2,0,1:T(8,128)(2,1)S(1)}, u32[]{:S(2)}, u32[]{:S(2)}) collective-permute-start(bf16[1,1,8,2048]{3,2,0,1:T(8,128)(2,1)S(1)} %get-tuple-element.177), channel_id=1, source_target_pairs={{0,2},{1,3},{2,4},{3,5},{4,6},{5,7},{6,8},{7,9},{8,10},{9,11},{10,... | collective-permute-start | bytes 98312 | tf_op jit(solution)/shard_map/ppermute | solution.py:123
  123.0 8.7 %collective-permute-start.2 = (bf16[1,1,8,2048]{3,2,0,1:T(8,128)(2,1)S(1)}, bf16[1,1,8,2048]{3,2,0,1:T(8,128)(2,1)S(1)}, u32[]{:S(2)}, u32[]{:S(2)}) collective-permute-start(bf16[1,1,8,2048]{3,2,0,1:T(8,128)(2,1)S(1)} %get-tuple-element.176), channel_id=1, source_target_pairs={{0,3},{1,4},{2,5},{3,6},{4,7},{5,8},{6,9},{7,10},{8,11},{9,12},{10... | collective-permute-start | bytes 98312 | tf_op jit(solution)/shard_map/ppermute | solution.py:123
  125.0 8.6 %collective-permute-start.3 = (bf16[1,1,8,2048]{3,2,0,1:T(8,128)(2,1)S(1)}, bf16[1,1,8,2048]{3,2,0,1:T(8,128)(2,1)S(1)}, u32[]{:S(2)}, u32[]{:S(2)}) collective-permute-start(bf16[1,1,8,2048]{3,2,0,1:T(8,128)(2,1)S(1)} %get-tuple-element.175), channel_id=1, source_target_pairs={{0,4},{1,5},{2,6},{3,7},{4,8},{5,9},{6,10},{7,11},{8,12},{9,13},{1... | collective-permute-start | bytes 98312 | tf_op jit(solution)/shard_map/ppermute | solution.py:123
  126.2 7.5 %collective-permute-start.4 = (bf16[1,1,8,2048]{3,2,0,1:T(8,128)(2,1)S(1)}, bf16[1,1,8,2048]{3,2,0,1:T(8,128)(2,1)S(1)}, u32[]{:S(2)}, u32[]{:S(2)}) collective-permute-start(bf16[1,1,8,2048]{3,2,0,1:T(8,128)(2,1)S(1)} %get-tuple-element.174), channel_id=1, source_target_pairs={{0,5},{1,6},{2,7},{3,8},{4,9},{5,10},{6,11},{7,12},{8,13},{9,14},{... | collective-permute-start | bytes 98312 | tf_op jit(solution)/shard_map/ppermute | solution.py:123
  128.1 7.1 %collective-permute-start.5 = (bf16[1,1,8,2048]{3,2,0,1:T(8,128)(2,1)S(1)}, bf16[1,1,8,2048]{3,2,0,1:T(8,128)(2,1)S(1)}, u32[]{:S(2)}, u32[]{:S(2)}) collective-permute-start(bf16[1,1,8,2048]{3,2,0,1:T(8,128)(2,1)S(1)} %get-tuple-element.173), channel_id=1, source_target_pairs={{0,6},{1,7},{2,8},{3,9},{4,10},{5,11},{6,12},{7,13},{8,14},{9,15},... | collective-permute-start | bytes 98312 | tf_op jit(solution)/shard_map/ppermute | solution.py:123
  129.1 9.7 %collective-permute-start.6 = (bf16[1,1,8,2048]{3,2,0,1:T(8,128)(2,1)S(1)}, bf16[1,1,8,2048]{3,2,0,1:T(8,128)(2,1)S(1)}, u32[]{:S(2)}, u32[]{:S(2)}) collective-permute-start(bf16[1,1,8,2048]{3,2,0,1:T(8,128)(2,1)S(1)} %get-tuple-element.172), channel_id=1, source_target_pairs={{0,7},{1,8},{2,9},{3,10},{4,11},{5,12},{6,13},{7,14},{8,15},{9,0},... | collective-permute-start | bytes 98312 | tf_op jit(solution)/shard_map/ppermute | solution.py:123
  131.8 7.7 %collective-permute-start.7 = (bf16[1,1,8,2048]{3,2,0,1:T(8,128)(2,1)S(1)}, bf16[1,1,8,2048]{3,2,0,1:T(8,128)(2,1)S(1)}, u32[]{:S(2)}, u32[]{:S(2)}) collective-permute-start(bf16[1,1,8,2048]{3,2,0,1:T(8,128)(2,1)S(1)} %get-tuple-element.171), channel_id=1, source_target_pairs={{0,8},{1,9},{2,10},{3,11},{4,12},{5,13},{6,14},{7,15},{8,0},{9,1},... | collective-permute-start | bytes 98312 | tf_op jit(solution)/shard_map/ppermute | solution.py:123
  133.6 6.5 %collective-permute-start.8 = (bf16[1,1,8,2048]{3,2,0,1:T(8,128)(2,1)S(1)}, bf16[1,1,8,2048]{3,2,0,1:T(8,128)(2,1)S(1)}, u32[]{:S(2)}, u32[]{:S(2)}) collective-permute-start(bf16[1,1,8,2048]{3,2,0,1:T(8,128)(2,1)S(1)} %get-tuple-element.170), channel_id=1, source_target_pairs={{0,9},{1,10},{2,11},{3,12},{4,13},{5,14},{6,15},{7,0},{8,1},{9,2},... | collective-permute-start | bytes 98312 | tf_op jit(solution)/shard_map/ppermute | solution.py:123
  133.7 8.4 %collective-permute-start.9 = (bf16[1,1,8,2048]{3,2,0,1:T(8,128)(2,1)S(1)}, bf16[1,1,8,2048]{3,2,0,1:T(8,128)(2,1)S(1)}, u32[]{:S(2)}, u32[]{:S(2)}) collective-permute-start(bf16[1,1,8,2048]{3,2,0,1:T(8,128)(2,1)S(1)} %get-tuple-element.169), channel_id=1, source_target_pairs={{0,10},{1,11},{2,12},{3,13},{4,14},{5,15},{6,0},{7,1},{8,2},{9,3},... | collective-permute-start | bytes 98312 | tf_op jit(solution)/shard_map/ppermute | solution.py:123
  135.2 9.6 %collective-permute-start.10 = (bf16[1,1,8,2048]{3,2,0,1:T(8,128)(2,1)S(1)}, bf16[1,1,8,2048]{3,2,0,1:T(8,128)(2,1)S(1)}, u32[]{:S(2)}, u32[]{:S(2)}) collective-permute-start(bf16[1,1,8,2048]{3,2,0,1:T(8,128)(2,1)S(1)} %get-tuple-element.168), channel_id=1, source_target_pairs={{0,11},{1,12},{2,13},{3,14},{4,15},{5,0},{6,1},{7,2},{8,3},{9,4},{... | collective-permute-start | bytes 98312 | tf_op jit(solution)/shard_map/ppermute | solution.py:123
  138.7 6.1 %collective-permute-start.11 = (bf16[1,1,8,2048]{3,2,0,1:T(8,128)(2,1)S(1)}, bf16[1,1,8,2048]{3,2,0,1:T(8,128)(2,1)S(1)}, u32[]{:S(2)}, u32[]{:S(2)}) collective-permute-start(bf16[1,1,8,2048]{3,2,0,1:T(8,128)(2,1)S(1)} %get-tuple-element.167), channel_id=1, source_target_pairs={{0,12},{1,13},{2,14},{3,15},{4,0},{5,1},{6,2},{7,3},{8,4},{9,5},{1... | collective-permute-start | bytes 98312 | tf_op jit(solution)/shard_map/ppermute | solution.py:123
  139.5 5.4 %collective-permute-start.12 = (bf16[1,1,8,2048]{3,2,0,1:T(8,128)(2,1)S(1)}, bf16[1,1,8,2048]{3,2,0,1:T(8,128)(2,1)S(1)}, u32[]{:S(2)}, u32[]{:S(2)}) collective-permute-start(bf16[1,1,8,2048]{3,2,0,1:T(8,128)(2,1)S(1)} %get-tuple-element.166), channel_id=1, source_target_pairs={{0,13},{1,14},{2,15},{3,0},{4,1},{5,2},{6,3},{7,4},{8,5},{9,6},{10... | collective-permute-start | bytes 98312 | tf_op jit(solution)/shard_map/ppermute | solution.py:123
  140.1 4.8 %collective-permute-start.13 = (bf16[1,1,8,2048]{3,2,0,1:T(8,128)(2,1)S(1)}, bf16[1,1,8,2048]{3,2,0,1:T(8,128)(2,1)S(1)}, u32[]{:S(2)}, u32[]{:S(2)}) collective-permute-start(bf16[1,1,8,2048]{3,2,0,1:T(8,128)(2,1)S(1)} %get-tuple-element.165), channel_id=1, source_target_pairs={{0,14},{1,15},{2,0},{3,1},{4,2},{5,3},{6,4},{7,5},{8,6},{9,7},{10,... | collective-permute-start | bytes 98312 | tf_op jit(solution)/shard_map/ppermute | solution.py:123
  142.1 4.3 %collective-permute-start.14 = (bf16[1,1,8,2048]{3,2,0,1:T(8,128)(2,1)S(1)}, bf16[1,1,8,2048]{3,2,0,1:T(8,128)(2,1)S(1)}, u32[]{:S(2)}, u32[]{:S(2)}) collective-permute-start(bf16[1,1,8,2048]{3,2,0,1:T(8,128)(2,1)S(1)} %get-tuple-element.164), channel_id=1, source_target_pairs={{0,15},{1,0},{2,1},{3,2},{4,3},{5,4},{6,5},{7,6},{8,7},{9,8},{10,9... | collective-permute-start | bytes 98312 | tf_op jit(solution)/shard_map/ppermute | solution.py:123
  148.2 3.5 %copy-start.2 = (bf16[1024,2048]{1,0:T(8,128)(2,1)S(1)}, bf16[1024,2048]{1,0:T(8,128)(2,1)}, u32[]{:S(2)}) copy-start(bf16[1024,2048]{1,0:T(8,128)(2,1)} %param.26) | copy-start | bytes 12582916
  153.2 3.5 %copy-start.3 = (bf16[1024,2048]{1,0:T(8,128)(2,1)S(1)}, bf16[1024,2048]{1,0:T(8,128)(2,1)}, u32[]{:S(2)}) copy-start(bf16[1024,2048]{1,0:T(8,128)(2,1)} %param.26) | copy-start | bytes 12582916
  158.2 3.5 %copy-start.4 = (bf16[1024,2048]{1,0:T(8,128)(2,1)S(1)}, bf16[1024,2048]{1,0:T(8,128)(2,1)}, u32[]{:S(2)}) copy-start(bf16[1024,2048]{1,0:T(8,128)(2,1)} %param.26) | copy-start | bytes 12582916
  161.8 1.7 %copy-start.7 = (bf16[128,1024]{1,0:T(8,128)(2,1)S(1)}, bf16[128,1024]{1,0:T(8,128)(2,1)}, u32[]{:S(2)}) copy-start(bf16[128,1024]{1,0:T(8,128)(2,1)} %copy-done.6) | copy-start | bytes 786436
  (1 other events, 0.9 us)
Sparse Core Ops, SparseCore 0:
  12.6 77.2 all-gather.3
